TPU v7x, 32 devices: a whole 2x2x4 slice. The times are simulated.
32 devices in a mesh: box: 8 (over y, x, core), sub: 4 (over z).
Axes of the slice: x: 2, y: 2, z: 4, core: 2. Of those that a mesh axis runs over, the one named last changes fastest.
Arguments:
- fine_state: float32 [8, 5, 8, 4096], P('box', None, 'sub'), as said below
- coarse_state: float32 [5, 4, 256, 128], P(None, 'sub', 'box'), as said below
- box_y: int32 [8], P('box'), may hold values from 1 to 95
Outputs:
- fine_next: float32 [8, 5, 8, 4096], P('box', None, 'sub')
- coarse_next: float32 [5, 4, 256, 128], P(None, 'sub', 'box')
Inputs may be any that keep to these rules, and one draw needn't show every extreme that they name: `fine_state`: density and pressure of every cell are positive. `coarse_state`: density and pressure of every cell are positive.
All inputs are finite; a program needn't handle non-finite values.
Results may differ from a plain program's by a relative error of at most 0.00002.
Values sent between devices are 32-bit elements; how exact they have to be, the bound alone decides.
A program may use at most 64 MiB of HBM per device.

v0:
```python
import functools

import jax
import jax.numpy as jnp
from jax import lax
from jax.experimental import pallas as pl
from jax.experimental.pallas import tpu as pltpu
from jax.sharding import PartitionSpec as P

MESH = pl.DeviceIdType.MESH
COMPS = 5


def primitives(state):
    inverse = 1.0 / state[0]
    velocity = [m * inverse for m in state[1:4]]
    kinetic = 0.5 * (
        state[1] * velocity[0] + state[2] * velocity[1] + state[3] * velocity[2]
    )
    pressure = 0.4 * (state[4] - kinetic)
    sound = jnp.sqrt(1.4 * pressure * inverse)
    return velocity, pressure, sound


def speed(state):
    velocity, _, sound = primitives(state)
    return jnp.abs(velocity[0]) + jnp.abs(velocity[1]) + jnp.abs(velocity[2]) + 3.0 * sound


def physical(state, prims, along):
    velocity, pressure, _ = prims
    v = velocity[along]
    parts = [state[1 + along]]
    for comp in range(3):
        term = state[1 + comp] * v
        parts.append(term + pressure if comp == along else term)
    parts.append((state[4] + pressure) * v)
    return parts


def reach(prims, along):
    return jnp.abs(prims[0][along]) + prims[2]


def rusanov(left, right, along):
    pl_, pr = primitives(left), primitives(right)
    a = jnp.maximum(reach(pl_, along), reach(pr, along))
    fl, fr = physical(left, pl_, along), physical(right, pr, along)
    return [0.5 * (fl[c] + fr[c]) - 0.5 * a * (right[c] - left[c]) for c in range(COMPS)]


def top(values):
    return jnp.max(jnp.max(values, axis=0, keepdims=True), axis=1, keepdims=True)


def dot(a, b):
    return jnp.dot(a, b, precision=lax.Precision.HIGHEST, preferred_element_type=jnp.float32)


def advance(
    nb, ns, by_hbm, f4, c3, f2, u_ref, tot, base, gain, info,
    by_ref, c_ref, gl, gu, zl, zh, ch, fh, es, yg, fy,
    msg, slots, anchor, anchors, send_a, recv_a, send_h, recv_h, load,
):
    b = lax.axis_index("box")
    s = lax.axis_index("sub")
    rows, lanes = u_ref.shape[1:]
    crows = c_ref.shape[1]
    last_f = f4.shape[1] - 1
    layers = f4.shape[2]
    edge = lanes // 2
    half = edge // 2
    barrier = pltpu.get_barrier_semaphore()
    count = nb * ns
    unroll = count <= 64
    me = b * ns + s

    def peer(k):
        other = lax.rem(me + k, count)
        return (lax.div(other, ns), lax.rem(other, ns))

    def hail(k, carry):
        pl.semaphore_signal(barrier, inc=1, device_id=peer(k), device_id_type=MESH)
        return carry

    load_u = pltpu.make_async_copy(f2, u_ref, load.at[0])
    load_c = pltpu.make_async_copy(c3, c_ref, load.at[1])
    lax.fori_loop(1, count, hail, 0, unroll=unroll)
    load_by = pltpu.make_async_copy(by_hbm, by_ref, load.at[2])
    load_c.start()
    load_u.start()
    load_by.start()
    load_c.wait()
    C = [c_ref[c] for c in range(COMPS)]
    coarse_top = top(speed(C))
    load_u.wait()
    U = [u_ref[c] for c in range(COMPS)]
    fine_top = top(speed(U))
    load_by.wait()
    by = by_ref[0]
    local = jnp.broadcast_to(jnp.maximum(fine_top, coarse_top), (1, lanes))
    msg[...] = local
    anchor[...] = jnp.full((8, lanes), by.astype(jnp.float32))

    for c in range(COMPS):
        zl[c] = u_ref[c, pl.ds(0, crows, stride=2)]
        zh[c] = u_ref[c, pl.ds(1, crows, stride=2)]

    pl.semaphore_wait(barrier, count - 1)

    def remote(src, dst, send, recv, peer):
        return pltpu.make_async_remote_copy(
            src_ref=src, dst_ref=dst, send_sem=send, recv_sem=recv,
            device_id=peer, device_id_type=MESH,
        )

    def tell(k, carry):
        remote(msg, slots.at[pl.ds(k - 1, 1)], send_a, recv_a, peer(k)).start()
        return carry

    lax.fori_loop(1, count, tell, 0, unroll=unroll)

    after, before = peer(ns), peer(count - ns)
    halos = [
        remote(c3.at[:, crows - 1], ch.at[0], send_h.at[0], recv_h.at[0], after),
        remote(c3.at[:, 0], ch.at[1], send_h.at[1], recv_h.at[1], before),
        remote(f4.at[:, last_f], fh.at[0], send_h.at[2], recv_h.at[2], after),
        remote(f4.at[:, 0], fh.at[1], send_h.at[3], recv_h.at[3], before),
        remote(anchor, anchors.at[0], send_h.at[6], recv_h.at[8], after),
        remote(anchor, anchors.at[1], send_h.at[7], recv_h.at[9], before),
    ]
    for copy in halos:
        copy.start()
    up = remote(
        zh, gl, send_h.at[4], recv_h.at[4],
        (b, jnp.minimum(s + 1, ns - 1)),
    )
    down = remote(
        zl, gu, send_h.at[5], recv_h.at[5], (b, jnp.maximum(s - 1, 0))
    )
    own_low = pltpu.make_async_copy(f4.at[:, :, 0], gl, recv_h.at[6])
    own_high = pltpu.make_async_copy(f4.at[:, :, layers - 1], gu, recv_h.at[7])
    pl.when(s < ns - 1)(up.start)
    pl.when(s > 0)(down.start)
    pl.when(s == 0)(own_low.start)
    pl.when(s == ns - 1)(own_high.start)

    sub_i = lax.broadcasted_iota(jnp.int32, (lanes, lanes), 0)
    lane_i = lax.broadcasted_iota(jnp.int32, (lanes, lanes), 1)
    spread_y = (lane_i & (edge - 1)) >> 1
    gather_y = (sub_i & (edge - 1)) >> 1

    def spread(anchor):
        return jnp.where(sub_i == anchor + spread_y, 1.0, 0.0)

    def pool(anchor, weight, keep):
        return jnp.where((lane_i == anchor + gather_y) & keep, weight, 0.0)

    r = lax.broadcasted_iota(jnp.int32, (rows, lanes), 0)
    lane = lax.broadcasted_iota(jnp.int32, (rows, lanes), 1)
    y = lane & (edge - 1)
    odd_l = (r & 1) == 1
    odd_x = lane >= edge
    odd_y = (lane & 1) == 1
    prims = primitives(U)
    clane = lax.broadcasted_iota(jnp.int32, (crows, lanes), 1)
    crow = lax.broadcasted_iota(jnp.int32, (crows, lanes), 0)
    at = clane & (edge - 1)
    for c in range(COMPS):
        low = jnp.sum(jnp.where(clane == by - 1, C[c], 0.0), axis=1, keepdims=True)
        high = jnp.sum(jnp.where(clane == by + half, C[c], 0.0), axis=1, keepdims=True)
        value = jnp.where(at == 0, low, high)
        yg[c, pl.ds(0, crows, stride=2)] = value
        yg[c, pl.ds(1, crows, stride=2)] = value

    def side(total, partner, along, sign):
        pp = primitives(partner)
        a = jnp.maximum(reach(prims, along), reach(pp, along))
        fp = physical(partner, pp, along)
        out = [sign * fp[c] + a * (U[c] - partner[c]) for c in range(COMPS)]
        if total is not None:
            out = [total[c] + out[c] for c in range(COMPS)]
        return out, a, fp

    sz = jnp.where(odd_l, 1.0, -1.0)
    sx = jnp.where(odd_x, 1.0, -1.0)
    sy = jnp.where(odd_y, 1.0, -1.0)
    inner = [
        jnp.where(odd_l, pltpu.roll(u, 1, 0), pltpu.roll(u, rows - 1, 0)) for u in U
    ]
    total, _, _ = side(None, inner, 0, -sz)
    inner = [pltpu.roll(u, edge, 1) for u in U]
    total, _, _ = side(total, inner, 1, -sx)
    low = [pltpu.roll(u, 1, 1) for u in U]
    high = [pltpu.roll(u, lanes - 1, 1) for u in U]
    inner = [jnp.where(odd_y, low[c], high[c]) for c in range(COMPS)]
    total, _, _ = side(total, inner, 2, -sy)
    rim = (y == 0) | (y == edge - 1)
    outer = [
        jnp.where(rim, yg[c], jnp.where(odd_y, high[c], low[c])) for c in range(COMPS)
    ]
    total, a, fp = side(total, outer, 2, sy)
    fu = physical(U, prims, 2)
    for c in range(COMPS):
        fy[c] = 0.5 * (fu[c] + fp[c]) + 0.5 * a * sy * (U[c] - outer[c])
        tot[c] = total[c]
    for c in range(COMPS):
        es[32 + c * crows : 32 + (c + 1) * crows] = (
            u_ref[c, pl.ds(0, crows, stride=2)] + u_ref[c, pl.ds(1, crows, stride=2)]
        )
    pool_own = pool(by, 0.125, sub_i >= 0)
    average = dot(es[32:], pool_own)
    covered = (clane >= by) & (clane < by + half)
    for c in range(COMPS):
        base[c] = jnp.where(covered, average[c * crows : (c + 1) * crows], C[c])

    cy = rusanov(C, [pltpu.roll(v, lanes - 1, 1) for v in C], 2)
    for c in range(COMPS):
        pair = fy[c, pl.ds(0, crows, stride=2)] + fy[c, pl.ds(1, crows, stride=2)]
        ff_lo = 0.25 * jnp.sum(jnp.where(at == 0, pair, 0.0), axis=1, keepdims=True)
        ff_hi = 0.25 * jnp.sum(jnp.where(at == edge - 1, pair, 0.0), axis=1, keepdims=True)
        gain[c] = jnp.where(clane == by - 1, cy[c] - ff_lo, 0.0) + jnp.where(
            clane == by + half, ff_hi - pltpu.roll(cy[c], 1, 1), 0.0
        )

    for copy in halos:
        copy.wait()
    by_prev = anchors[0, 0:1, :].astype(jnp.int32)
    by_next = anchors[1, 0:1, :].astype(jnp.int32)
    for c in range(COMPS):
        es[c : c + 1] = c_ref[c, 0:1]
        es[8 + c : 9 + c] = c_ref[c, crows - 1 : crows]
        es[16 + c : 17 + c] = ch[0, c : c + 1]
        es[24 + c : 25 + c] = ch[1, c : c + 1]
    ghost_x = dot(es[16:32], spread(by))
    own_up_prev = dot(es[0:8], spread(by_prev))
    own_up_next = dot(es[8:16], spread(by_next))

    total = [tot[c] for c in range(COMPS)]
    outer = []
    for c in range(COMPS):
        v = pltpu.roll(U[c], edge, 1)
        g = jnp.where(odd_x, pltpu.roll(v, rows - 2, 0), pltpu.roll(v, 2, 0))
        g = jnp.where((r < 2) & ~odd_x, ghost_x[c : c + 1], g)
        g = jnp.where((r >= rows - 2) & odd_x, ghost_x[8 + c : 9 + c], g)
        outer.append(g)
    total, _, _ = side(total, outer, 1, sx)

    split = lambda v, k: [v[k + c : k + c + 1] for c in range(COMPS)]
    own_lo, own_hi, prev, nxt = (split(es[0:32], k) for k in (0, 8, 16, 24))
    fine_prev = [fh[0, c] for c in range(COMPS)]
    fine_next = [fh[1, c] for c in range(COMPS)]
    wide = lambda v: [jnp.broadcast_to(w, fine_prev[0].shape) for w in v]
    ff_prev = rusanov(fine_prev, wide(split(own_up_prev, 0)), 1)
    ff_next = rusanov(wide(split(own_up_next, 0)), fine_next, 1)
    fc_prev = rusanov(prev, own_lo, 1)
    fc_next = rusanov(own_hi, nxt, 1)
    for c in range(COMPS):
        es[c : c + 1] = jnp.sum(ff_prev[c], axis=0, keepdims=True)
        es[8 + c : 9 + c] = jnp.sum(ff_next[c], axis=0, keepdims=True)
    upper_half = sub_i >= edge
    pooled_prev = dot(es[0:8], pool(by_prev, 0.25, upper_half))
    pooled_next = dot(es[8:16], pool(by_next, 0.25, ~upper_half))
    one = lax.broadcasted_iota(jnp.int32, (1, lanes), 1)
    in_prev = (one >= by_prev) & (one < by_prev + half)
    in_next = (one >= by_next) & (one < by_next + half)

    pl.when(s > 0)(up.wait_recv)
    pl.when(s < ns - 1)(down.wait_recv)
    pl.when(s == 0)(own_low.wait)
    pl.when(s == ns - 1)(own_high.wait)
    for c in range(COMPS):
        yg[c, pl.ds(0, crows, stride=2)] = gl[c]
        yg[c, pl.ds(1, crows, stride=2)] = gu[c]
    total, _, _ = side(total, [yg[c] for c in range(COMPS)], 0, sz)
    for c in range(COMPS):
        tot[c] = total[c]

    for c in range(COMPS):
        es[32 + c * crows : 32 + (c + 1) * crows] = (
            tot[c, pl.ds(0, crows, stride=2)] + tot[c, pl.ds(1, crows, stride=2)]
        )
    average = dot(es[32:], pool_own)
    for c in range(COMPS):
        low = jnp.where(in_prev, pooled_prev[c : c + 1] - fc_prev[c], 0.0)
        high = jnp.where(in_next, fc_next[c] - pooled_next[c : c + 1], 0.0)
        out = gain[c] + jnp.where(crow == 0, low, 0.0)
        out = out + jnp.where(crow == crows - 1, high, 0.0)
        gain[c] = jnp.where(covered, -average[c * crows : (c + 1) * crows], out)

    told = slots.at[pl.ds(0, count - 1)]
    pltpu.make_async_copy(told, told, recv_a).wait()
    srow = lax.broadcasted_iota(jnp.int32, slots.shape, 0)
    merged = jnp.max(jnp.where(srow < count - 1, slots[...], local), axis=0, keepdims=True)
    info[...] = jnp.broadcast_to(merged, info.shape)
    pl.when(s < ns - 1)(up.wait_send)
    pl.when(s > 0)(down.wait_send)
    pltpu.make_async_copy(told, told, send_a).wait()


def finish(u_ref, tot, base, gain, info, fo, co):
    hdt = 0.5 * (0.8 / info[0:1, :])
    for c in range(COMPS):
        fo[c] = u_ref[c] - hdt * tot[c]
        co[c] = base[c] + hdt * gain[c]


def shards(nb, ns, fine_state, coarse_state, box_y):
    layers, cells = fine_state.shape[2:]
    lanes = coarse_state.shape[3]
    crows = coarse_state.shape[2]
    blocks = cells // lanes
    rows = blocks * layers
    f4 = fine_state[0].reshape(COMPS, layers, blocks, lanes).transpose(0, 2, 1, 3)
    f2 = f4.reshape(COMPS, rows, lanes)
    c3 = coarse_state.reshape(COMPS, crows, lanes)
    f32 = lambda *shape: jax.ShapeDtypeStruct(shape, jnp.float32)
    buf = lambda *shape: pltpu.VMEM(shape, jnp.float32)
    vmem = pl.BlockSpec(memory_space=pltpu.VMEM)
    hbm = pl.BlockSpec(memory_space=pltpu.HBM)
    fine = (COMPS, rows, lanes)
    coarse = (COMPS, crows, lanes)
    dma = pltpu.SemaphoreType.DMA
    u, tot, base, gain, info = pl.pallas_call(
        functools.partial(advance, nb, ns),
        out_shape=(buf(*fine), buf(*fine), buf(*coarse), buf(*coarse), buf(8, lanes)),
        in_specs=[hbm, hbm, hbm, hbm],
        out_specs=(vmem,) * 5,
        scratch_shapes=[
            pltpu.SMEM((1,), jnp.int32), buf(*coarse), buf(*coarse), buf(*coarse),
            buf(*coarse), buf(*coarse),
            buf(2, COMPS, lanes), buf(2, COMPS, layers, lanes),
            buf(32 + COMPS * crows, lanes), buf(*fine), buf(*fine),
            buf(1, lanes), buf(nb * ns, lanes), buf(8, lanes), buf(2, 8, lanes),
            dma, dma, dma((8,)), dma((10,)), dma((3,)),
        ],
        compiler_params=pltpu.CompilerParams(collective_id=0, has_side_effects=True),
        name="advance",
    )(box_y, f4, c3, f2)
    fo, co = pl.pallas_call(
        finish,
        out_shape=(f32(*fine), f32(*coarse)),
        in_specs=[vmem] * 5,
        out_specs=(vmem, vmem),
        name="finish",
    )(*(pltpu.with_memory_space_constraint(v, pltpu.VMEM) for v in (u, tot, base, gain, info)))
    fresh = fo.reshape(COMPS, blocks, layers, lanes).transpose(0, 2, 1, 3)
    return fresh.reshape(1, COMPS, layers, cells), co.reshape(coarse_state.shape)


def solution(mesh):
    placed = (P("box", None, "sub", None), P(None, "sub", "box", None), P("box"))
    return jax.shard_map(
        functools.partial(shards, mesh.shape["box"], mesh.shape["sub"]),
        mesh=mesh,
        in_specs=placed,
        out_specs=(P("box", None, "sub", None), P(None, "sub", "box", None)),
        check_vma=False,
    )
```

profile of v0, /device:TPU:0, one launch (start us, length us, event | category | flops | bytes accessed | tf_op | source)
XLA Modules:
  0.0 13.4 jit_solution(9890151729960722329)
XLA Ops:
  1.3 11.4 %advance.1 = (f32[5,64,128]{2,1,0:T(8,128)S(1)}, f32[5,64,128]{2,1,0:T(8,128)S(1)}, f32[5,32,128]{2,1,0:T(8,128)S(1)}, f32[5,32,128]{2,1,0:T(8,128)S(1)}, f32[8,128]{1,0:T(8,128)S(1)}) custom-call(s32[1]{0:T(128)S(6)} %copy.7.by_hbm, f32[5,32,2,128]{3,2,1,0:T(2,128)} %bitcast.14, f32[5,32,128]{2,1,0:T(8,128)} %bitcast.16, f32[5,64,128]{2,1,0:T(8,128)} %bitcast.15), custom_call_target="tpu_custom_call" | custom-call | tf_op jit(solution)/shard_map/advance/pallas_call | solution.py:324
  12.7 0.7 %finish.1 = (f32[5,64,128]{2,1,0:T(8,128)}, f32[5,32,128]{2,1,0:T(8,128)}) custom-call(f32[5,64,128]{2,1,0:T(8,128)S(1)} %get-tuple-element.9.u_ref, f32[5,64,128]{2,1,0:T(8,128)S(1)} %get-tuple-element.10.tot, f32[5,32,128]{2,1,0:T(8,128)S(1)} %get-tuple-element.11.base, f32[5,32,128]{2,1,0:T(8,128)S(1)} %get-tuple-element.12.gain, ...), custom_call_target="tpu_custom_call" | custom-call | tf_op jit(solution)/shard_map/finish/pallas_call | solution.py:340
where the time goes:
time: 13.5 us; the launch traced here: 13.4 us
  Pallas kernels  12.1 us (90%)
  between operations  1.28 us (9%)
    pallas_call x1, Pallas kernels, shards(): pl.pallas_call(functools.partial(advance, nb, ns), out_shape=(buf(*fine),...  11.4 us
    pallas_call x1, Pallas kernels, shards(): pl.pallas_call(finish, out_shape=(f32(*fine), f32(*coarse)), in_specs=[vm...  0.72 us

commit v1 on v0

--- a/solution.py
+++ b/solution.py
@@ -60,7 +60,7 @@
 def advance(
     nb, ns, by_hbm, f4, c3, f2, u_ref, tot, base, gain, info,
     by_ref, c_ref, gl, gu, zl, zh, ch, fh, es, yg, fy,
-    msg, slots, anchor, anchors, send_a, recv_a, send_h, recv_h, load,
+    msg, slots, anchor, anchors, send_a, recv_a, send_h, recv_h, load, go,
 ):
     b = lax.axis_index("box")
     s = lax.axis_index("sub")
@@ -73,40 +73,61 @@
     barrier = pltpu.get_barrier_semaphore()
     count = nb * ns
     unroll = count <= 64
-    me = b * ns + s
+    hub = (b == nb - 1) & (s == ns - 1)
+    inner_s = (s > 0) & (s < ns - 1)
 
     def peer(k):
-        other = lax.rem(me + k, count)
-        return (lax.div(other, ns), lax.rem(other, ns))
-
-    def hail(k, carry):
-        pl.semaphore_signal(barrier, inc=1, device_id=peer(k), device_id_type=MESH)
-        return carry
+        return (lax.rem(b + lax.rem(k, nb), nb), lax.rem(s + lax.div(k, nb), ns))
+
+    def signal(sem, device):
+        pl.semaphore_signal(sem, inc=1, device_id=device, device_id_type=MESH)
 
     load_u = pltpu.make_async_copy(f2, u_ref, load.at[0])
     load_c = pltpu.make_async_copy(c3, c_ref, load.at[1])
-    lax.fori_loop(1, count, hail, 0, unroll=unroll)
     load_by = pltpu.make_async_copy(by_hbm, by_ref, load.at[2])
     load_c.start()
     load_u.start()
     load_by.start()
+
+    pl.when((s < ns - 2) | ((s == ns - 2) & (b < nb - 1)))(
+        lambda: signal(barrier, (nb - 1, ns - 1))
+    )
+    pl.when(s > 0)(lambda: signal(barrier, (b, s - 1)))
+    pl.when(s < ns - 1)(lambda: signal(barrier, (b, s + 1)))
+
+    def hail(k, carry):
+        signal(barrier, peer(k))
+        return carry
+
+    def release(k, carry):
+        signal(go, peer(k))
+        return carry
+
+    lax.fori_loop(1, nb, hail, 0, unroll=unroll)
+
+    @pl.when(hub)
+    def _():
+        pl.semaphore_wait(barrier, count - 1)
+        lax.fori_loop(1, count, release, 0, unroll=unroll)
+
     load_c.wait()
     C = [c_ref[c] for c in range(COMPS)]
     coarse_top = top(speed(C))
     load_u.wait()
     U = [u_ref[c] for c in range(COMPS)]
     fine_top = top(speed(U))
+    local = jnp.broadcast_to(jnp.maximum(fine_top, coarse_top), (1, lanes))
+    msg[...] = local
     load_by.wait()
     by = by_ref[0]
-    local = jnp.broadcast_to(jnp.maximum(fine_top, coarse_top), (1, lanes))
-    msg[...] = local
     anchor[...] = jnp.full((8, lanes), by.astype(jnp.float32))
 
     for c in range(COMPS):
         zl[c] = u_ref[c, pl.ds(0, crows, stride=2)]
         zh[c] = u_ref[c, pl.ds(1, crows, stride=2)]
 
-    pl.semaphore_wait(barrier, count - 1)
+    pl.when(inner_s)(lambda: pl.semaphore_wait(barrier, nb + 1))
+    pl.when(~inner_s & ~hub)(lambda: pl.semaphore_wait(barrier, nb))
 
     def remote(src, dst, send, recv, peer):
         return pltpu.make_async_remote_copy(
@@ -118,9 +139,15 @@
         remote(msg, slots.at[pl.ds(k - 1, 1)], send_a, recv_a, peer(k)).start()
         return carry
 
-    lax.fori_loop(1, count, tell, 0, unroll=unroll)
-
-    after, before = peer(ns), peer(count - ns)
+    lax.fori_loop(1, nb, tell, 0, unroll=unroll)
+
+    def spread_far():
+        pl.when(~hub)(lambda: pl.semaphore_wait(go, 1))
+        lax.fori_loop(nb, count, tell, 0, unroll=unroll)
+
+    pl.when(2 * s >= ns)(spread_far)
+
+    after, before = peer(1), peer(nb - 1)
     halos = [
         remote(c3.at[:, crows - 1], ch.at[0], send_h.at[0], recv_h.at[0], after),
         remote(c3.at[:, 0], ch.at[1], send_h.at[1], recv_h.at[1], before),
@@ -223,6 +250,7 @@
             clane == by + half, ff_hi - pltpu.roll(cy[c], 1, 1), 0.0
         )
 
+    pl.when((2 * s < ns) & (s > 0))(spread_far)
     for copy in halos:
         copy.wait()
     by_prev = anchors[0, 0:1, :].astype(jnp.int32)
@@ -288,6 +316,7 @@
         out = out + jnp.where(crow == crows - 1, high, 0.0)
         gain[c] = jnp.where(covered, -average[c * crows : (c + 1) * crows], out)
 
+    pl.when((2 * s < ns) & (s == 0))(spread_far)
     told = slots.at[pl.ds(0, count - 1)]
     pltpu.make_async_copy(told, told, recv_a).wait()
     srow = lax.broadcasted_iota(jnp.int32, slots.shape, 0)
@@ -332,7 +361,7 @@
             buf(2, COMPS, lanes), buf(2, COMPS, layers, lanes),
             buf(32 + COMPS * crows, lanes), buf(*fine), buf(*fine),
             buf(1, lanes), buf(nb * ns, lanes), buf(8, lanes), buf(2, 8, lanes),
-            dma, dma, dma((8,)), dma((10,)), dma((3,)),
+            dma, dma, dma((8,)), dma((10,)), dma((3,)), pltpu.SemaphoreType.REGULAR,
         ],
         compiler_params=pltpu.CompilerParams(collective_id=0, has_side_effects=True),
         name="advance",

time: 13.5 us -> 12.6 us (0.933)
  Pallas kernels: 12.1 us -> 11.1 us
    pallas_call x1, Pallas kernels: 11.4 us -> 10.4 us  [shards(): pl.pallas_call(functools.partial(advance, nb, ns), out_shape=(buf(*fine),...]
where the time goes in v1:
time: 12.6 us; the launch traced here: 12.4 us
  Pallas kernels  11.1 us (88%)
  between operations  1.28 us (10%)
    pallas_call x1, Pallas kernels, shards(): pl.pallas_call(functools.partial(advance, nb, ns), out_shape=(buf(*fine),...  10.4 us
    pallas_call x1, Pallas kernels, shards(): pl.pallas_call(finish, out_shape=(f32(*fine), f32(*coarse)), in_specs=[vm...  0.72 us

profile of v1, /device:TPU:0, one launch (start us, length us, event | category | flops | bytes accessed | tf_op | source)
XLA Modules:
  0.0 12.4 jit_solution(5963382951069492536)
XLA Ops:
  1.3 10.4 %advance.1 = (f32[5,64,128]{2,1,0:T(8,128)S(1)}, f32[5,64,128]{2,1,0:T(8,128)S(1)}, f32[5,32,128]{2,1,0:T(8,128)S(1)}, f32[5,32,128]{2,1,0:T(8,128)S(1)}, f32[8,128]{1,0:T(8,128)S(1)}) custom-call(s32[1]{0:T(128)S(6)} %copy.7.by_hbm, f32[5,32,2,128]{3,2,1,0:T(2,128)} %bitcast.14, f32[5,32,128]{2,1,0:T(8,128)} %bitcast.16, f32[5,64,128]{2,1,0:T(8,128)} %bitcast.15), custom_call_target="tpu_custom_call" | custom-call | tf_op jit(solution)/shard_map/advance/pallas_call | solution.py:353
  11.7 0.7 %finish.1 = (f32[5,64,128]{2,1,0:T(8,128)}, f32[5,32,128]{2,1,0:T(8,128)}) custom-call(f32[5,64,128]{2,1,0:T(8,128)S(1)} %get-tuple-element.9.u_ref, f32[5,64,128]{2,1,0:T(8,128)S(1)} %get-tuple-element.10.tot, f32[5,32,128]{2,1,0:T(8,128)S(1)} %get-tuple-element.11.base, f32[5,32,128]{2,1,0:T(8,128)S(1)} %get-tuple-element.12.gain, ...), custom_call_target="tpu_custom_call" | custom-call | tf_op jit(solution)/shard_map/finish/pallas_call | solution.py:369

commit v2 on v1

--- a/solution.py
+++ b/solution.py
@@ -73,11 +73,12 @@
     barrier = pltpu.get_barrier_semaphore()
     count = nb * ns
     unroll = count <= 64
-    hub = (b == nb - 1) & (s == ns - 1)
-    inner_s = (s > 0) & (s < ns - 1)
+    last_s = s == ns - 1
 
     def peer(k):
         return (lax.rem(b + lax.rem(k, nb), nb), lax.rem(s + lax.div(k, nb), ns))
+
+    above = nb * (ns - s)
 
     def signal(sem, device):
         pl.semaphore_signal(sem, inc=1, device_id=device, device_id_type=MESH)
@@ -89,26 +90,12 @@
     load_u.start()
     load_by.start()
 
-    pl.when((s < ns - 2) | ((s == ns - 2) & (b < nb - 1)))(
-        lambda: signal(barrier, (nb - 1, ns - 1))
-    )
-    pl.when(s > 0)(lambda: signal(barrier, (b, s - 1)))
-    pl.when(s < ns - 1)(lambda: signal(barrier, (b, s + 1)))
-
     def hail(k, carry):
         signal(barrier, peer(k))
         return carry
 
-    def release(k, carry):
-        signal(go, peer(k))
-        return carry
-
-    lax.fori_loop(1, nb, hail, 0, unroll=unroll)
-
-    @pl.when(hub)
-    def _():
-        pl.semaphore_wait(barrier, count - 1)
-        lax.fori_loop(1, count, release, 0, unroll=unroll)
+    pl.when(s > 0)(lambda: signal(barrier, (b, s - 1)))
+    lax.fori_loop(1, above, hail, 0)
 
     load_c.wait()
     C = [c_ref[c] for c in range(COMPS)]
@@ -126,8 +113,14 @@
         zl[c] = u_ref[c, pl.ds(0, crows, stride=2)]
         zh[c] = u_ref[c, pl.ds(1, crows, stride=2)]
 
-    pl.when(inner_s)(lambda: pl.semaphore_wait(barrier, nb + 1))
-    pl.when(~inner_s & ~hub)(lambda: pl.semaphore_wait(barrier, nb))
+    heard = nb * (s + 1) - 1
+    pl.when(last_s)(lambda: pl.semaphore_wait(barrier, heard))
+    pl.when(~last_s)(lambda: pl.semaphore_wait(barrier, heard + 1))
+
+    @pl.when(last_s)
+    def _():
+        for j in range(ns - 1):
+            signal(go, (b, j))
 
     def remote(src, dst, send, recv, peer):
         return pltpu.make_async_remote_copy(
@@ -139,13 +132,12 @@
         remote(msg, slots.at[pl.ds(k - 1, 1)], send_a, recv_a, peer(k)).start()
         return carry
 
+    lax.fori_loop(above, count, tell, 0)
     lax.fori_loop(1, nb, tell, 0, unroll=unroll)
 
-    def spread_far():
-        pl.when(~hub)(lambda: pl.semaphore_wait(go, 1))
-        lax.fori_loop(nb, count, tell, 0, unroll=unroll)
-
-    pl.when(2 * s >= ns)(spread_far)
+    def spread_up():
+        pl.semaphore_wait(go, 1)
+        lax.fori_loop(nb, above, tell, 0)
 
     after, before = peer(1), peer(nb - 1)
     halos = [
@@ -250,7 +242,7 @@
             clane == by + half, ff_hi - pltpu.roll(cy[c], 1, 1), 0.0
         )
 
-    pl.when((2 * s < ns) & (s > 0))(spread_far)
+    pl.when(~last_s)(spread_up)
     for copy in halos:
         copy.wait()
     by_prev = anchors[0, 0:1, :].astype(jnp.int32)
@@ -316,7 +308,6 @@
         out = out + jnp.where(crow == crows - 1, high, 0.0)
         gain[c] = jnp.where(covered, -average[c * crows : (c + 1) * crows], out)
 
-    pl.when((2 * s < ns) & (s == 0))(spread_far)
     told = slots.at[pl.ds(0, count - 1)]
     pltpu.make_async_copy(told, told, recv_a).wait()
     srow = lax.broadcasted_iota(jnp.int32, slots.shape, 0)

time: 12.6 us -> 12.1 us (0.960)
  Pallas kernels: 11.1 us -> 10.7 us
    pallas_call x1, Pallas kernels: 10.4 us -> 9.98 us  [shards(): pl.pallas_call(functools.partial(advance, nb, ns), out_shape=(buf(*fine),...]
where the time goes in v2:
time: 12.1 us; the launch traced here: 12 us
  Pallas kernels  10.7 us (88%)
  between operations  1.28 us (11%)
    pallas_call x1, Pallas kernels, shards(): pl.pallas_call(functools.partial(advance, nb, ns), out_shape=(buf(*fine),...  9.98 us
    pallas_call x1, Pallas kernels, shards(): pl.pallas_call(finish, out_shape=(f32(*fine), f32(*coarse)), in_specs=[vm...  0.72 us

profile of v2, /device:TPU:0, one launch (start us, length us, event | category | flops | bytes accessed | tf_op | source)
XLA Modules:
  0.0 12.0 jit_solution(8415951197857748381)
XLA Ops:
  1.3 10.0 %advance.1 = (f32[5,64,128]{2,1,0:T(8,128)S(1)}, f32[5,64,128]{2,1,0:T(8,128)S(1)}, f32[5,32,128]{2,1,0:T(8,128)S(1)}, f32[5,32,128]{2,1,0:T(8,128)S(1)}, f32[8,128]{1,0:T(8,128)S(1)}) custom-call(s32[1]{0:T(128)S(6)} %copy.7.by_hbm, f32[5,32,2,128]{3,2,1,0:T(2,128)} %bitcast.14, f32[5,32,128]{2,1,0:T(8,128)} %bitcast.16, f32[5,64,128]{2,1,0:T(8,128)} %bitcast.15), custom_call_target="tpu_custom_call" | custom-call | tf_op jit(solution)/shard_map/advance/pallas_call | solution.py:344
  11.3 0.7 %finish.1 = (f32[5,64,128]{2,1,0:T(8,128)}, f32[5,32,128]{2,1,0:T(8,128)}) custom-call(f32[5,64,128]{2,1,0:T(8,128)S(1)} %get-tuple-element.9.u_ref, f32[5,64,128]{2,1,0:T(8,128)S(1)} %get-tuple-element.10.tot, f32[5,32,128]{2,1,0:T(8,128)S(1)} %get-tuple-element.11.base, f32[5,32,128]{2,1,0:T(8,128)S(1)} %get-tuple-element.12.gain, ...), custom_call_target="tpu_custom_call" | custom-call | tf_op jit(solution)/shard_map/finish/pallas_call | solution.py:360

commit v3 on v2

--- a/solution.py
+++ b/solution.py
@@ -58,8 +58,8 @@
 
 
 def advance(
-    nb, ns, by_hbm, f4, c3, f2, u_ref, tot, base, gain, info,
-    by_ref, c_ref, gl, gu, zl, zh, ch, fh, es, yg, fy,
+    nb, ns, by_ref, f4, c3, f2, u_ref, tot, base, gain, info,
+    c_ref, gl, gu, zl, zh, ch, fh, es, yg, fy,
     msg, slots, anchor, anchors, send_a, recv_a, send_h, recv_h, load, go,
 ):
     b = lax.axis_index("box")
@@ -85,10 +85,8 @@
 
     load_u = pltpu.make_async_copy(f2, u_ref, load.at[0])
     load_c = pltpu.make_async_copy(c3, c_ref, load.at[1])
-    load_by = pltpu.make_async_copy(by_hbm, by_ref, load.at[2])
     load_c.start()
     load_u.start()
-    load_by.start()
 
     def hail(k, carry):
         signal(barrier, peer(k))
@@ -99,13 +97,14 @@
 
     load_c.wait()
     C = [c_ref[c] for c in range(COMPS)]
-    coarse_top = top(speed(C))
+    coarse_top = speed(C)
     load_u.wait()
     U = [u_ref[c] for c in range(COMPS)]
-    fine_top = top(speed(U))
-    local = jnp.broadcast_to(jnp.maximum(fine_top, coarse_top), (1, lanes))
+    fine_top = speed(U)
+    for k in range(0, rows, crows):
+        coarse_top = jnp.maximum(coarse_top, fine_top[k : k + crows])
+    local = jnp.broadcast_to(top(coarse_top), (1, lanes))
     msg[...] = local
-    load_by.wait()
     by = by_ref[0]
     anchor[...] = jnp.full((8, lanes), by.astype(jnp.float32))
 
@@ -309,13 +308,13 @@
         gain[c] = jnp.where(covered, -average[c * crows : (c + 1) * crows], out)
 
     told = slots.at[pl.ds(0, count - 1)]
+    pl.when(s < ns - 1)(up.wait_send)
+    pl.when(s > 0)(down.wait_send)
+    pltpu.make_async_copy(told, told, send_a).wait()
     pltpu.make_async_copy(told, told, recv_a).wait()
     srow = lax.broadcasted_iota(jnp.int32, slots.shape, 0)
     merged = jnp.max(jnp.where(srow < count - 1, slots[...], local), axis=0, keepdims=True)
     info[...] = jnp.broadcast_to(merged, info.shape)
-    pl.when(s < ns - 1)(up.wait_send)
-    pl.when(s > 0)(down.wait_send)
-    pltpu.make_async_copy(told, told, send_a).wait()
 
 
 def finish(u_ref, tot, base, gain, info, fo, co):
@@ -344,15 +343,15 @@
     u, tot, base, gain, info = pl.pallas_call(
         functools.partial(advance, nb, ns),
         out_shape=(buf(*fine), buf(*fine), buf(*coarse), buf(*coarse), buf(8, lanes)),
-        in_specs=[hbm, hbm, hbm, hbm],
+        in_specs=[pl.BlockSpec(memory_space=pltpu.SMEM), hbm, hbm, hbm],
         out_specs=(vmem,) * 5,
         scratch_shapes=[
-            pltpu.SMEM((1,), jnp.int32), buf(*coarse), buf(*coarse), buf(*coarse),
+            buf(*coarse), buf(*coarse), buf(*coarse),
             buf(*coarse), buf(*coarse),
             buf(2, COMPS, lanes), buf(2, COMPS, layers, lanes),
             buf(32 + COMPS * crows, lanes), buf(*fine), buf(*fine),
             buf(1, lanes), buf(nb * ns, lanes), buf(8, lanes), buf(2, 8, lanes),
-            dma, dma, dma((8,)), dma((10,)), dma((3,)), pltpu.SemaphoreType.REGULAR,
+            dma, dma, dma((8,)), dma((10,)), dma((2,)), pltpu.SemaphoreType.REGULAR,
         ],
         compiler_params=pltpu.CompilerParams(collective_id=0, has_side_effects=True),
         name="advance",

time: 12.1 us -> 12 us (level)
    pallas_call x1, Pallas kernels: 9.98 us -> 9.85 us  [shards(): pl.pallas_call(functools.partial(advance, nb, ns), out_shape=(buf(*fine),...]
where the time goes in v3:
time: 12 us; the launch traced here: 11.9 us
  Pallas kernels  10.6 us (88%)
  between operations  1.28 us (11%)
    pallas_call x1, Pallas kernels, shards(): pl.pallas_call(functools.partial(advance, nb, ns), out_shape=(buf(*fine),...  9.85 us
    pallas_call x1, Pallas kernels, shards(): pl.pallas_call(finish, out_shape=(f32(*fine), f32(*coarse)), in_specs=[vm...  0.72 us

profile of v3, /device:TPU:0, one launch (start us, length us, event | category | flops | bytes accessed | tf_op | source)
XLA Modules:
  0.0 11.9 jit_solution(13367817344225283969)
XLA Ops:
  1.3 9.9 %advance.1 = (f32[5,64,128]{2,1,0:T(8,128)S(1)}, f32[5,64,128]{2,1,0:T(8,128)S(1)}, f32[5,32,128]{2,1,0:T(8,128)S(1)}, f32[5,32,128]{2,1,0:T(8,128)S(1)}, f32[8,128]{1,0:T(8,128)S(1)}) custom-call(s32[1]{0:T(128)S(6)} %copy.7.by_ref, f32[5,32,2,128]{3,2,1,0:T(2,128)} %bitcast.14, f32[5,32,128]{2,1,0:T(8,128)} %bitcast.16, f32[5,64,128]{2,1,0:T(8,128)} %bitcast.15), custom_call_target="tpu_custom_call" | custom-call | tf_op jit(solution)/shard_map/advance/pallas_call | solution.py:343
  11.1 0.7 %finish.1 = (f32[5,64,128]{2,1,0:T(8,128)}, f32[5,32,128]{2,1,0:T(8,128)}) custom-call(f32[5,64,128]{2,1,0:T(8,128)S(1)} %get-tuple-element.9.u_ref, f32[5,64,128]{2,1,0:T(8,128)S(1)} %get-tuple-element.10.tot, f32[5,32,128]{2,1,0:T(8,128)S(1)} %get-tuple-element.11.base, f32[5,32,128]{2,1,0:T(8,128)S(1)} %get-tuple-element.12.gain, ...), custom_call_target="tpu_custom_call" | custom-call | tf_op jit(solution)/shard_map/finish/pallas_call | solution.py:359
